TPU v7x, 128 devices: a whole 4x4x4 slice. The times are simulated.
128 devices in a mesh: section: 2 (over x_lo), seq: 8 (over y, core), tp: 8 (over z, x_hi).
Axes of the slice: x: 4 (x_hi: 2, x_lo: 2; x = x_hi * 2 + x_lo), y: 4, z: 4, core: 2. Of those that a mesh axis runs over, the one named last changes fastest.
Arguments:
- hidden_image: bfloat16 [2, 1024, 1536], P(None, 'seq'), may hold values from -6 to 6
- hidden_text: bfloat16 [2, 256, 1536], P(None, 'seq'), may hold values from -6 to 6
- latent: float32 [2, 1024, 64], P(None, 'seq'), may hold values from -6 to 6
- timestep: int32 [2], replicated, may hold values from 14 to 27
- text_length: int32 [2], replicated, may hold values from 64 to 154, as said below
- text_keep: int32 [2, 256], replicated, may hold values 0 or 1
- patch_order: int32 [4], replicated, may hold values from 0 to 3, each once
- stale_image_kv: bfloat16 [2, 2, 1024, 2, 1536], P('section', None, 'seq', None, 'tp'), may hold values from -160 to 160
- stale_text_kv: bfloat16 [2, 2, 256, 2, 1536], P('section', None, 'seq', None, 'tp'), may hold values from -6 to 6
- mod_image: float32 [2, 2, 6, 1536], P('section'), may hold values from -3 to 3
- mod_text: float32 [2, 2, 6, 1536], P('section'), may hold values from -3 to 3
- mod_final: float32 [2, 2, 1536], replicated, may hold values from -3 to 3
- qkv_image: bfloat16 [2, 1536, 3, 1536], P('section', None, None, 'tp'), may hold values from -0.15625 to 0.15625
- out_image: bfloat16 [2, 1536, 1536], P('section', 'tp'), may hold values from -0.15625 to 0.15625
- up_image: bfloat16 [2, 1536, 6144], P('section', None, 'tp'), may hold values from -0.15625 to 0.15625
- down_image: bfloat16 [2, 6144, 1536], P('section', 'tp'), may hold values from -0.078125 to 0.078125
- qkv_text: bfloat16 [2, 1536, 3, 1536], P('section', None, None, 'tp'), may hold values from -0.15625 to 0.15625
- out_text: bfloat16 [2, 1536, 1536], P('section', 'tp'), may hold values from -0.15625 to 0.15625
- up_text: bfloat16 [2, 1536, 6144], P('section', None, 'tp'), may hold values from -0.15625 to 0.15625
- down_text: bfloat16 [2, 6144, 1536], P('section', 'tp'), may hold values from -0.078125 to 0.078125
- final_weight: bfloat16 [1536, 64], replicated, may hold values from -0.3125 to 0.3125
Outputs:
- latent_out: float32 [2, 2, 1024, 64], P('section', None, 'seq')
- image_kv_next: bfloat16 [2, 2, 1024, 2, 1536], P('section', None, 'seq', None, 'tp')
- text_kv_next: bfloat16 [2, 2, 256, 2, 1536], P('section', None, 'seq', None, 'tp')
- text_hidden: bfloat16 [2, 2, 256, 1536], P('section', None, 'seq')
Inputs may be any that keep to these rules, and one draw needn't show every extreme that they name: `text_length`: some request has exactly 154 text tokens.
All inputs are finite; a program needn't handle non-finite values.
Results may differ from a plain program's by a relative error of at most 0.023.
Values may be sent and summed in bfloat16 or wider, within the bound.
No kernel may reach another device: no remote copies, remote signals or barrier semaphores. Data moves between devices by JAX's collectives and lax.ppermute only.
A program may use at most 128 MiB of HBM per device.

v0:
```python
import jax
import jax.numpy as jnp
from jax import lax
from jax.sharding import PartitionSpec as P

HD = 64
STEPS = 28
EPSILON = 1e-06
NEGATIVE = -1e30
TIME_SHIFT = 3.0


def passed_along(value, axis, steps):
    count = lax.axis_size(axis)
    initial, last = (max(0, -steps), min(count, count - steps))
    return lax.ppermute(value, axis, [(source, source + steps) for source in range(initial, last)])


def row_norm(values, shift_rows, scale_rows):
    mean_value = jnp.mean(values, axis=-1, keepdims=True)
    centred = values - mean_value
    variance = jnp.mean(centred * centred, axis=-1, keepdims=True)
    return centred * lax.rsqrt(variance + EPSILON) * (1.0 + scale_rows) + shift_rows


def expand_rows(vectors, row_count):
    return jnp.broadcast_to(
        vectors[:, None, :], (vectors.shape[0], row_count, vectors.shape[1])
    ).reshape(-1, vectors.shape[1])


def project(rows, shift_rows, scale_rows, weight):
    flattened = rows.reshape(-1, rows.shape[-1]).astype(jnp.float32)
    normed = row_norm(flattened, shift_rows, scale_rows).astype(jnp.bfloat16)
    mixed = jnp.dot(
        normed, weight.reshape(weight.shape[0], -1), preferred_element_type=jnp.float32
    ).astype(jnp.bfloat16)
    return mixed.reshape(rows.shape[0], rows.shape[1], 3, -1)


def split_heads(values):
    return values.reshape(values.shape[0], values.shape[1], -1, HD)


def block_scores(queries, keys_block, key_mask):
    scores = jnp.einsum(
        "rqhe,rkhe->rhqk", queries, keys_block, preferred_element_type=jnp.float32
    ) * HD ** (-0.5)
    return jnp.where(key_mask[:, None, None, :], scores, NEGATIVE)


def block_weights(scores, rowmax, values_block, key_mask):
    exponent = jnp.where(key_mask[:, None, None, :], jnp.exp(scores - rowmax[..., None]), 0.0)
    totals = jnp.sum(exponent, axis=-1)
    summed = jnp.einsum(
        "rhqk,rkhe->rhqe",
        exponent.astype(jnp.bfloat16),
        values_block,
        preferred_element_type=jnp.float32,
    )
    return (totals, summed)


def heads_out(totals, summed):
    result = summed / totals[..., None]
    merged = jnp.transpose(result, (0, 2, 1, 3))
    return merged.reshape(result.shape[0], result.shape[2], -1).astype(jnp.bfloat16)


def sigma_of(index_value):
    progress = 1.0 - index_value / STEPS
    return TIME_SHIFT * progress / (1.0 + (TIME_SHIFT - 1.0) * progress)


def on_device(
    hidden_image,
    hidden_text,
    latent,
    timestep,
    text_length,
    text_keep,
    patch_order,
    stale_image_kv,
    stale_text_kv,
    mod_image,
    mod_text,
    mod_final,
    qkv_image,
    out_image,
    up_image,
    down_image,
    qkv_text,
    out_text,
    up_text,
    down_text,
    final_weight,
):
    requests = hidden_image.shape[0]
    model_width = hidden_image.shape[2]
    slot_count = patch_order.shape[0]
    image_local = hidden_image.shape[1]
    text_local = hidden_text.shape[1]
    patch_rows = image_local // slot_count
    group_rows = text_local // slot_count
    slot_rows = patch_rows + group_rows
    local_width = qkv_image.shape[3]
    seq_count = lax.axis_size("seq")
    section_index = lax.axis_index("section")
    first_section = section_index == 0
    text_total = text_keep.shape[1]
    positions = jnp.arange(text_total, dtype=jnp.int32)
    valid_text = (positions[None, :] < text_length[:, None]) & (text_keep == 1)
    stale_image, stale_text = (
        lax.all_gather(stale_image_kv[0], "seq", axis=1, tiled=True),
        lax.all_gather(stale_text_kv[0], "seq", axis=1, tiled=True),
    )
    image_buffer = stale_image.reshape(requests, seq_count, slot_count, patch_rows, 2, local_width)
    text_buffer = stale_text.reshape(requests, seq_count, slot_count, group_rows, 2, local_width)
    image_mrows = [expand_rows(mod_image[0][:, column], patch_rows) for column in range(6)]
    text_mrows = [expand_rows(mod_text[0][:, column], group_rows) for column in range(6)]
    image_input = hidden_image.reshape(requests, slot_count, patch_rows, model_width)
    text_input = hidden_text.reshape(requests, slot_count, group_rows, model_width)
    image_store = jnp.zeros((requests, slot_count, patch_rows, model_width), jnp.bfloat16)
    text_store = jnp.zeros((requests, slot_count, group_rows, model_width), jnp.bfloat16)
    image_kv_store = jnp.zeros((requests, slot_count, patch_rows, 2, local_width), jnp.bfloat16)
    text_kv_store = jnp.zeros((requests, slot_count, group_rows, 2, local_width), jnp.bfloat16)
    arrived_image = jnp.zeros((requests, patch_rows, model_width), jnp.bfloat16)
    arrived_text = jnp.zeros((requests, group_rows, model_width), jnp.bfloat16)
    for moment in range(slot_count + 1):
        slot_raw = moment - section_index
        in_range = (slot_raw >= 0) & (slot_raw < slot_count)
        slot_index = jnp.clip(slot_raw, 0, slot_count - 1)
        patch_index = lax.dynamic_index_in_dim(patch_order, slot_index, 0, keepdims=False)
        image_rows = jnp.where(
            first_section,
            lax.dynamic_index_in_dim(image_input, patch_index, 1, keepdims=False),
            arrived_image,
        )
        text_rows = jnp.where(
            first_section,
            lax.dynamic_index_in_dim(text_input, slot_index, 1, keepdims=False),
            arrived_text,
        )
        image_qkv = project(image_rows, image_mrows[0], image_mrows[1], qkv_image[0])
        text_qkv = project(text_rows, text_mrows[0], text_mrows[1], qkv_text[0])
        fresh_local = jnp.concatenate([image_qkv[:, :, 1:], text_qkv[:, :, 1:]], axis=1)
        queries = split_heads(jnp.concatenate([image_qkv[:, :, 0], text_qkv[:, :, 0]], axis=1))
        fresh_all = lax.all_gather(fresh_local, "seq", axis=1, tiled=True)
        fresh_split = fresh_all.reshape(requests, seq_count, slot_rows, 2, local_width)
        image_buffer = lax.dynamic_update_slice_in_dim(
            image_buffer, fresh_split[:, :, None, :patch_rows], patch_index, axis=2
        )
        text_buffer = lax.dynamic_update_slice_in_dim(
            text_buffer, fresh_split[:, :, None, patch_rows:], slot_index, axis=2
        )
        image_keys = image_buffer.reshape(requests, -1, 2, local_width)
        text_keys = text_buffer.reshape(requests, -1, 2, local_width)
        image_mask = jnp.ones((requests, image_keys.shape[1]), jnp.bool_)
        image_scores = block_scores(queries, split_heads(image_keys[:, :, 0]), image_mask)
        text_scores = block_scores(queries, split_heads(text_keys[:, :, 0]), valid_text)
        rowmax = jnp.maximum(jnp.max(image_scores, axis=-1), jnp.max(text_scores, axis=-1))
        image_totals, image_summed = block_weights(
            image_scores, rowmax, split_heads(image_keys[:, :, 1]), image_mask
        )
        text_totals, text_summed = block_weights(
            text_scores, rowmax, split_heads(text_keys[:, :, 1]), valid_text
        )
        attended = heads_out(image_totals + text_totals, image_summed + text_summed)
        image_part = jnp.dot(
            attended[:, :patch_rows].reshape(-1, local_width),
            out_image[0],
            preferred_element_type=jnp.float32,
        )
        text_part = jnp.dot(
            attended[:, patch_rows:].reshape(-1, local_width),
            out_text[0],
            preferred_element_type=jnp.float32,
        )
        image_flat = image_rows.reshape(-1, model_width).astype(jnp.float32)
        text_flat = text_rows.reshape(-1, model_width).astype(jnp.float32)
        image_sum, text_sum = (
            lax.psum(image_part.astype(jnp.bfloat16), "tp").astype(jnp.float32),
            lax.psum(text_part.astype(jnp.bfloat16), "tp").astype(jnp.float32),
        )
        image_first = image_flat + image_mrows[2] * image_sum
        text_first = text_flat + text_mrows[2] * text_sum
        image_normed = row_norm(image_first, image_mrows[3], image_mrows[4]).astype(jnp.bfloat16)
        text_normed = row_norm(text_first, text_mrows[3], text_mrows[4]).astype(jnp.bfloat16)
        image_hidden = jax.nn.gelu(
            jnp.dot(image_normed, up_image[0], preferred_element_type=jnp.float32), approximate=True
        ).astype(jnp.bfloat16)
        text_hidden_rows = jax.nn.gelu(
            jnp.dot(text_normed, up_text[0], preferred_element_type=jnp.float32), approximate=True
        ).astype(jnp.bfloat16)
        image_down, text_down = (
            lax.psum(
                jnp.dot(image_hidden, down_image[0], preferred_element_type=jnp.float32).astype(
                    jnp.bfloat16
                ),
                "tp",
            ).astype(jnp.float32),
            lax.psum(
                jnp.dot(text_hidden_rows, down_text[0], preferred_element_type=jnp.float32).astype(
                    jnp.bfloat16
                ),
                "tp",
            ).astype(jnp.float32),
        )
        image_new = (image_first + image_mrows[5] * image_down).astype(jnp.bfloat16)
        text_new = (text_first + text_mrows[5] * text_down).astype(jnp.bfloat16)
        image_new_rows = image_new.reshape(requests, patch_rows, model_width)
        text_new_rows = text_new.reshape(requests, group_rows, model_width)
        image_store = jnp.where(
            in_range,
            lax.dynamic_update_index_in_dim(image_store, image_new_rows, patch_index, 1),
            image_store,
        )
        text_store = jnp.where(
            in_range,
            lax.dynamic_update_index_in_dim(text_store, text_new_rows, slot_index, 1),
            text_store,
        )
        image_kv_store = jnp.where(
            in_range,
            lax.dynamic_update_index_in_dim(image_kv_store, image_qkv[:, :, 1:], patch_index, 1),
            image_kv_store,
        )
        text_kv_store = jnp.where(
            in_range,
            lax.dynamic_update_index_in_dim(text_kv_store, text_qkv[:, :, 1:], slot_index, 1),
            text_kv_store,
        )
        if moment < slot_count:
            arrived_image, arrived_text = passed_along(
                (image_new_rows, text_new_rows), "section", 1
            )
    final_rows = image_store.reshape(-1, model_width).astype(jnp.float32)
    final_normed = row_norm(
        final_rows,
        expand_rows(mod_final[:, 0], image_local),
        expand_rows(mod_final[:, 1], image_local),
    ).astype(jnp.bfloat16)
    velocity = jnp.dot(final_normed, final_weight, preferred_element_type=jnp.float32).reshape(
        requests, image_local, -1
    )
    returned = passed_along(velocity.astype(jnp.bfloat16), "section", -1).astype(velocity.dtype)
    velocity_used = jnp.where(first_section, returned, velocity)
    index_value = timestep.astype(jnp.float32)
    sigma_now = sigma_of(index_value)
    sigma_next = sigma_of(index_value + 1.0)
    stepped = latent + (sigma_next - sigma_now)[:, None, None] * velocity_used
    denoised = latent - sigma_now[:, None, None] * velocity_used
    latent_part = jnp.where(first_section, stepped, denoised)[None]
    return (
        latent_part,
        image_kv_store.reshape(requests, image_local, 2, local_width)[None],
        text_kv_store.reshape(requests, text_local, 2, local_width)[None],
        text_store.reshape(requests, text_local, model_width)[None],
    )


def solution(mesh):
    in_specs = (
        P(None, "seq", None),
        P(None, "seq", None),
        P(None, "seq", None),
        P(),
        P(),
        P(),
        P(),
        P("section", None, "seq", None, "tp"),
        P("section", None, "seq", None, "tp"),
        P("section", None, None, None),
        P("section", None, None, None),
        P(),
        P("section", None, None, "tp"),
        P("section", "tp", None),
        P("section", None, "tp"),
        P("section", "tp", None),
        P("section", None, None, "tp"),
        P("section", "tp", None),
        P("section", None, "tp"),
        P("section", "tp", None),
        P(),
    )
    out_specs = (
        P("section", None, "seq", None),
        P("section", None, "seq", None, "tp"),
        P("section", None, "seq", None, "tp"),
        P("section", None, "seq", None),
    )
    return jax.shard_map(
        on_device, mesh=mesh, in_specs=in_specs, out_specs=out_specs, check_vma=False
    )
```

profile of v0, /device:TPU:2, one launch (start us, length us, event | category | flops | bytes accessed | tf_op | source)
XLA Modules:
  0.0 1606.8 jit_solution(7978806751904991760)
XLA Ops:
  25.3 14.3 all-gather.1
  40.6 13.2 all_gather.22
  81.3 3.0 fusion.598
  87.8 2.3 copy.295
  94.2 42.6 %psum.142 = bf16[16,1536]{1,0:T(8,128)(2,1)S(1)} all-reduce(bf16[16,1536]{1,0:T(8,128)(2,1)S(1)} %convolution_convert_fusion.9), channel_id=1, replica_groups=mesh['section'=2,'seq'=8,'tp'=8] {'tp'}, use_global_device_ids=true, to_apply=%region_14.15 | all-reduce | flops 24576 | bytes 98304 | tf_op jit(solution)/shard_map/psum | solution.py:183
  137.2 3.4 fusion.55
  140.6 38.1 %psum.143 = bf16[16,1536]{1,0:T(8,128)(2,1)} all-reduce(bf16[16,1536]{1,0:T(8,128)(2,1)S(1)} %fusion.55), channel_id=1, replica_groups=mesh['section'=2,'seq'=8,'tp'=8] {'tp'}, use_global_device_ids=true, to_apply=%region_17.18 | all-reduce | flops 24576 | bytes 98304 | tf_op jit(solution)/shard_map/psum | solution.py:202
  183.3 3.2 collective-permute-done.1
  191.2 77.5 %all-reduce.11.cloned.1.call-done = bf16[64,1536]{1,0:T(8,128)(2,1)} async-done(((bf16[64,1536]{1,0:T(8,128)(2,1)}), bf16[64,1536]{1,0:T(8,128)(2,1)}) %all-reduce.11.cloned.1.call-update) | async-done | bytes 196624 | tf_op jit(solution)/shard_map/psum | solution.py:182
  272.8 3.6 fusion.40
  276.6 81.9 %all-reduce.13.cloned.1.call-done = bf16[64,1536]{1,0:T(8,128)(2,1)} async-done(((bf16[64,1536]{1,0:T(8,128)(2,1)}), bf16[64,1536]{1,0:T(8,128)(2,1)}) %all-reduce.13.cloned.1.call-update) | async-done | bytes 196624 | tf_op jit(solution)/shard_map/psum | solution.py:196
  361.6 5.7 collective-permute-done
  372.8 13.6 all_gather.24
  396.4 3.0 fusion.597
  414.5 39.5 %psum.146 = bf16[16,1536]{1,0:T(8,128)(2,1)S(1)} all-reduce(bf16[16,1536]{1,0:T(8,128)(2,1)S(1)} %convolution_convert_fusion.8), channel_id=1, replica_groups=mesh['section'=2,'seq'=8,'tp'=8] {'tp'}, use_global_device_ids=true, to_apply=%region_30.31 | all-reduce | flops 24576 | bytes 98304 | tf_op jit(solution)/shard_map/psum | solution.py:183
  454.4 4.0 fusion.58
  458.4 40.0 %psum.147 = bf16[16,1536]{1,0:T(8,128)(2,1)} all-reduce(bf16[16,1536]{1,0:T(8,128)(2,1)} %fusion.58), channel_id=1, replica_groups=mesh['section'=2,'seq'=8,'tp'=8] {'tp'}, use_global_device_ids=true, to_apply=%region_33.34 | all-reduce | flops 24576 | bytes 98304 | tf_op jit(solution)/shard_map/psum | solution.py:202
  510.7 77.7 %all-reduce.15.cloned.1.call-done = bf16[64,1536]{1,0:T(8,128)(2,1)} async-done(((bf16[64,1536]{1,0:T(8,128)(2,1)}), bf16[64,1536]{1,0:T(8,128)(2,1)}) %all-reduce.15.cloned.1.call-update) | async-done | bytes 196624 | tf_op jit(solution)/shard_map/psum | solution.py:182
  592.5 3.6 fusion.43
  597.5 80.7 %all-reduce.17.cloned.1.call-done = bf16[64,1536]{1,0:T(8,128)(2,1)} async-done(((bf16[64,1536]{1,0:T(8,128)(2,1)}), bf16[64,1536]{1,0:T(8,128)(2,1)}) %all-reduce.17.cloned.1.call-update) | async-done | bytes 196624 | tf_op jit(solution)/shard_map/psum | solution.py:196
  680.8 6.2 collective-permute-done.2
  692.5 13.8 all_gather.25
  716.2 3.0 fusion.596
  734.4 39.5 %psum.150 = bf16[16,1536]{1,0:T(8,128)(2,1)S(1)} all-reduce(bf16[16,1536]{1,0:T(8,128)(2,1)S(1)} %convolution_convert_fusion.7), channel_id=1, replica_groups=mesh['section'=2,'seq'=8,'tp'=8] {'tp'}, use_global_device_ids=true, to_apply=%region_46.47 | all-reduce | flops 24576 | bytes 98304 | tf_op jit(solution)/shard_map/psum | solution.py:183
  774.3 4.0 fusion.61
  778.3 40.0 %psum.151 = bf16[16,1536]{1,0:T(8,128)(2,1)} all-reduce(bf16[16,1536]{1,0:T(8,128)(2,1)} %fusion.61), channel_id=1, replica_groups=mesh['section'=2,'seq'=8,'tp'=8] {'tp'}, use_global_device_ids=true, to_apply=%region_49.50 | all-reduce | flops 24576 | bytes 98304 | tf_op jit(solution)/shard_map/psum | solution.py:202
  830.6 77.7 %all-reduce.19.cloned.1.call-done = bf16[64,1536]{1,0:T(8,128)(2,1)} async-done(((bf16[64,1536]{1,0:T(8,128)(2,1)}), bf16[64,1536]{1,0:T(8,128)(2,1)}) %all-reduce.19.cloned.1.call-update) | async-done | bytes 196624 | tf_op jit(solution)/shard_map/psum | solution.py:182
  912.3 3.6 fusion.46
  917.3 80.7 %all-reduce.21.cloned.1.call-done = bf16[64,1536]{1,0:T(8,128)(2,1)} async-done(((bf16[64,1536]{1,0:T(8,128)(2,1)}), bf16[64,1536]{1,0:T(8,128)(2,1)}) %all-reduce.21.cloned.1.call-update) | async-done | bytes 196624 | tf_op jit(solution)/shard_map/psum | solution.py:196
  1000.6 6.2 collective-permute-done.4
  1012.3 13.6 all_gather.26
  1035.9 3.0 fusion.595
  1054.0 39.7 %psum.154 = bf16[16,1536]{1,0:T(8,128)(2,1)S(1)} all-reduce(bf16[16,1536]{1,0:T(8,128)(2,1)S(1)} %convolution_convert_fusion.6), channel_id=1, replica_groups=mesh['section'=2,'seq'=8,'tp'=8] {'tp'}, use_global_device_ids=true, to_apply=%region_62.63 | all-reduce | flops 24576 | bytes 98304 | tf_op jit(solution)/shard_map/psum | solution.py:183
  1094.1 4.0 fusion.64
  1098.2 40.0 %psum.155 = bf16[16,1536]{1,0:T(8,128)(2,1)} all-reduce(bf16[16,1536]{1,0:T(8,128)(2,1)} %fusion.64), channel_id=1, replica_groups=mesh['section'=2,'seq'=8,'tp'=8] {'tp'}, use_global_device_ids=true, to_apply=%region_65.66 | all-reduce | flops 24576 | bytes 98304 | tf_op jit(solution)/shard_map/psum | solution.py:202
  1149.1 79.0 %all-reduce.23.cloned.1.call-done = bf16[64,1536]{1,0:T(8,128)(2,1)} async-done(((bf16[64,1536]{1,0:T(8,128)(2,1)}), bf16[64,1536]{1,0:T(8,128)(2,1)}) %all-reduce.23.cloned.1.call-update) | async-done | bytes 196624 | tf_op jit(solution)/shard_map/psum | solution.py:182
  1232.2 3.6 fusion.49
  1238.0 79.9 %all-reduce.25.cloned.1.call-done = bf16[64,1536]{1,0:T(8,128)(2,1)} async-done(((bf16[64,1536]{1,0:T(8,128)(2,1)}), bf16[64,1536]{1,0:T(8,128)(2,1)}) %all-reduce.25.cloned.1.call-update) | async-done | bytes 196624 | tf_op jit(solution)/shard_map/psum | solution.py:196
  1320.5 6.2 collective-permute-done.6
  1332.2 13.6 all_gather.27
  1354.0 3.0 fusion.594
  1374.0 39.5 %psum.158 = bf16[16,1536]{1,0:T(8,128)(2,1)S(1)} all-reduce(bf16[16,1536]{1,0:T(8,128)(2,1)S(1)} %convolution_convert_fusion.5), channel_id=1, replica_groups=mesh['section'=2,'seq'=8,'tp'=8] {'tp'}, use_global_device_ids=true, to_apply=%region_78.79 | all-reduce | flops 24576 | bytes 98304 | tf_op jit(solution)/shard_map/psum | solution.py:183
  1415.9 4.0 fusion.67
  1419.9 39.8 %psum.159 = bf16[16,1536]{1,0:T(8,128)(2,1)} all-reduce(bf16[16,1536]{1,0:T(8,128)(2,1)} %fusion.67), channel_id=1, replica_groups=mesh['section'=2,'seq'=8,'tp'=8] {'tp'}, use_global_device_ids=true, to_apply=%region_81.82 | all-reduce | flops 24576 | bytes 98304 | tf_op jit(solution)/shard_map/psum | solution.py:202
  1459.7 36.9 %all-reduce.27.cloned.1.call-done = bf16[64,1536]{1,0:T(8,128)(2,1)} async-done(((bf16[64,1536]{1,0:T(8,128)(2,1)}), bf16[64,1536]{1,0:T(8,128)(2,1)}) %all-reduce.27.cloned.1.call-update) | async-done | bytes 196624 | tf_op jit(solution)/shard_map/psum | solution.py:182
  1500.7 3.6 fusion.52
  1505.8 80.6 %all-reduce.29.cloned.1.call-done = bf16[64,1536]{1,0:T(8,128)(2,1)} async-done(((bf16[64,1536]{1,0:T(8,128)(2,1)}), bf16[64,1536]{1,0:T(8,128)(2,1)}) %all-reduce.29.cloned.1.call-update) | async-done | bytes 196624 | tf_op jit(solution)/shard_map/psum | solution.py:196
  1591.9 3.4 collective-permute-start.8
  (567 shorter events, 262.4 us)
Async XLA Ops:
  7.2 265.6 %copy-start = (bf16[1,768,1536]{2,1,0:T(8,128)(2,1)S(1)}, bf16[1,768,1536]{2,1,0:T(8,128)(2,1)}, u32[]{:S(2)}) copy-start(bf16[1,768,1536]{2,1,0:T(8,128)(2,1)} %param.36) | copy-start | bytes 7077892
  7.2 73.1 %all-gather.4.cloned.1.call-start = ((), (), s32[]{:S(2)}) async-start(), calls=%async_computation.10 | async-start | bytes 2359296 | tf_op jit(solution)/shard_map/all_gather | solution.py:114
  9.2 259.5 %all-reduce.11.cloned.1.call-start = ((), (), s32[]{:S(2)}) async-start(), calls=%async_computation | async-start | bytes 393216 | tf_op jit(solution)/shard_map/psum | solution.py:182
  140.6 130.4 %copy-start.73 = (f32[2,1536]{1,0:T(2,128)S(1)}, f32[2,1536]{1,0:T(2,128)}, u32[]{:S(2)}) copy-start(f32[2,1536]{1,0:T(2,128)} %get-tuple-element.117) | copy-start | bytes 36868
  140.6 130.4 %copy-start.78 = (f32[2,1536]{1,0:T(2,128)S(1)}, f32[2,1536]{1,0:T(2,128)}, u32[]{:S(2)}) copy-start(f32[2,1536]{1,0:T(2,128)} %get-tuple-element.118) | copy-start | bytes 36868
  180.3 6.3 collective-permute-start.1
  183.2 85.5 %copy-start.12 = (bf16[2,128,1536]{2,1,0:T(8,128)(2,1)S(1)}, bf16[2,128,1536]{2,1,0:T(8,128)(2,1)}, u32[]{:S(2)}) copy-start(bf16[2,128,1536]{2,1,0:T(8,128)(2,1)} %param.21) | copy-start | bytes 2359300
  183.3 175.3 %all-reduce.13.cloned.1.call-start = ((), (), s32[]{:S(2)}) async-start(), calls=%async_computation.1 | async-start | bytes 393216 | tf_op jit(solution)/shard_map/psum | solution.py:196
  272.8 85.7 %copy-start.13 = (bf16[64,1536]{1,0:T(8,128)(2,1)S(1)}, bf16[64,1536]{1,0:T(8,128)(2,1)}, u32[]{:S(2)}) copy-start(bf16[64,1536]{1,0:T(8,128)(2,1)} %all-reduce.11.cloned.1.call-done) | copy-start | bytes 589828
  272.8 85.7 %copy-start.68 = (f32[2,1,1536]{2,0,1:T(2,128)S(1)}, f32[2,1,1536]{2,0,1:T(2,128)}, u32[]{:S(2)}) copy-start(f32[2,1,1536]{2,0,1:T(2,128)} %copy.408) | copy-start | bytes 36868
  276.4 92.2 %copy-start.59 = (f32[2,1536]{1,0:T(2,128)S(1)}, f32[2,1536]{1,0:T(2,128)}, u32[]{:S(2)}) copy-start(f32[2,1536]{1,0:T(2,128)} %copy-done.58) | copy-start | bytes 36868
  276.4 92.2 %copy-start.64 = (f32[2,1536]{1,0:T(2,128)S(1)}, f32[2,1536]{1,0:T(2,128)}, u32[]{:S(2)}) copy-start(f32[2,1536]{1,0:T(2,128)} %copy-done.63) | copy-start | bytes 36868
  276.5 312.0 %all-reduce.15.cloned.1.call-start = ((), (), s32[]{:S(2)}) async-start(), calls=%async_computation.2 | async-start | bytes 393216 | tf_op jit(solution)/shard_map/psum | solution.py:182
  276.6 92.2 %copy-start.27 = (bf16[2,4,8,2,192]{4,3,2,0,1:T(2,128)(2,1)}, bf16[2,4,8,2,192]{4,3,2,0,1:T(2,128)(2,1)S(1)}, u32[]{:S(2)}) copy-start(bf16[2,4,8,2,192]{4,3,2,0,1:T(2,128)(2,1)S(1)} %fusion.540) | copy-start | bytes 147460
  359.7 7.6 collective-permute-start
  458.4 132.2 %copy-start.74 = (f32[2,1536]{1,0:T(2,128)S(1)}, f32[2,1536]{1,0:T(2,128)}, u32[]{:S(2)}) copy-start(f32[2,1536]{1,0:T(2,128)} %get-tuple-element.117) | copy-start | bytes 36868
  458.4 132.3 %copy-start.79 = (f32[2,1536]{1,0:T(2,128)S(1)}, f32[2,1536]{1,0:T(2,128)}, u32[]{:S(2)}) copy-start(f32[2,1536]{1,0:T(2,128)} %get-tuple-element.118) | copy-start | bytes 36868
  499.9 6.2 collective-permute-start.3
  504.9 173.3 %all-reduce.17.cloned.1.call-start = ((), (), s32[]{:S(2)}) async-start(), calls=%async_computation.3 | async-start | bytes 393216 | tf_op jit(solution)/shard_map/psum | solution.py:196
  592.4 85.7 %copy-start.69 = (f32[2,1,1536]{2,0,1:T(2,128)S(1)}, f32[2,1,1536]{2,0,1:T(2,128)}, u32[]{:S(2)}) copy-start(f32[2,1,1536]{2,0,1:T(2,128)} %copy.408) | copy-start | bytes 36868
  596.1 92.2 %copy-start.60 = (f32[2,1536]{1,0:T(2,128)S(1)}, f32[2,1536]{1,0:T(2,128)}, u32[]{:S(2)}) copy-start(f32[2,1536]{1,0:T(2,128)} %copy-done.58) | copy-start | bytes 36868
  596.1 92.2 %copy-start.65 = (f32[2,1536]{1,0:T(2,128)S(1)}, f32[2,1536]{1,0:T(2,128)}, u32[]{:S(2)}) copy-start(f32[2,1536]{1,0:T(2,128)} %copy-done.63) | copy-start | bytes 36868
  596.1 312.2 %all-reduce.19.cloned.1.call-start = ((), (), s32[]{:S(2)}) async-start(), calls=%async_computation.4 | async-start | bytes 393216 | tf_op jit(solution)/shard_map/psum | solution.py:182
  679.4 7.6 collective-permute-start.2
  778.3 132.2 %copy-start.75 = (f32[2,1536]{1,0:T(2,128)S(1)}, f32[2,1536]{1,0:T(2,128)}, u32[]{:S(2)}) copy-start(f32[2,1536]{1,0:T(2,128)} %get-tuple-element.117) | copy-start | bytes 36868
  778.3 132.2 %copy-start.80 = (f32[2,1536]{1,0:T(2,128)S(1)}, f32[2,1536]{1,0:T(2,128)}, u32[]{:S(2)}) copy-start(f32[2,1536]{1,0:T(2,128)} %get-tuple-element.118) | copy-start | bytes 36868
  819.8 6.2 collective-permute-start.5
  824.7 173.2 %all-reduce.21.cloned.1.call-start = ((), (), s32[]{:S(2)}) async-start(), calls=%async_computation.5 | async-start | bytes 393216 | tf_op jit(solution)/shard_map/psum | solution.py:196
  912.3 85.7 %copy-start.70 = (f32[2,1,1536]{2,0,1:T(2,128)S(1)}, f32[2,1,1536]{2,0,1:T(2,128)}, u32[]{:S(2)}) copy-start(f32[2,1,1536]{2,0,1:T(2,128)} %copy.408) | copy-start | bytes 36868
  915.9 92.2 %copy-start.61 = (f32[2,1536]{1,0:T(2,128)S(1)}, f32[2,1536]{1,0:T(2,128)}, u32[]{:S(2)}) copy-start(f32[2,1536]{1,0:T(2,128)} %copy-done.58) | copy-start | bytes 36868
  915.9 92.2 %copy-start.66 = (f32[2,1536]{1,0:T(2,128)S(1)}, f32[2,1536]{1,0:T(2,128)}, u32[]{:S(2)}) copy-start(f32[2,1536]{1,0:T(2,128)} %copy-done.63) | copy-start | bytes 36868
  915.9 312.2 %all-reduce.23.cloned.1.call-start = ((), (), s32[]{:S(2)}) async-start(), calls=%async_computation.6 | async-start | bytes 393216 | tf_op jit(solution)/shard_map/psum | solution.py:182
  999.2 7.6 collective-permute-start.4
  1098.2 132.2 %copy-start.76 = (f32[2,1536]{1,0:T(2,128)S(1)}, f32[2,1536]{1,0:T(2,128)}, u32[]{:S(2)}) copy-start(f32[2,1536]{1,0:T(2,128)} %get-tuple-element.117) | copy-start | bytes 36868
  1098.2 132.2 %copy-start.81 = (f32[2,1536]{1,0:T(2,128)S(1)}, f32[2,1536]{1,0:T(2,128)}, u32[]{:S(2)}) copy-start(f32[2,1536]{1,0:T(2,128)} %get-tuple-element.118) | copy-start | bytes 36868
  1139.6 6.2 collective-permute-start.7
  1144.6 173.3 %all-reduce.25.cloned.1.call-start = ((), (), s32[]{:S(2)}) async-start(), calls=%async_computation.7 | async-start | bytes 393216 | tf_op jit(solution)/shard_map/psum | solution.py:196
  1232.2 85.7 %copy-start.71 = (f32[2,1,1536]{2,0,1:T(2,128)S(1)}, f32[2,1,1536]{2,0,1:T(2,128)}, u32[]{:S(2)}) copy-start(f32[2,1,1536]{2,0,1:T(2,128)} %copy.408) | copy-start | bytes 36868
  1235.8 92.2 %copy-start.62 = (f32[2,1536]{1,0:T(2,128)S(1)}, f32[2,1536]{1,0:T(2,128)}, u32[]{:S(2)}) copy-start(f32[2,1536]{1,0:T(2,128)} %copy-done.58) | copy-start | bytes 36868
  1235.8 92.2 %copy-start.67 = (f32[2,1536]{1,0:T(2,128)S(1)}, f32[2,1536]{1,0:T(2,128)}, u32[]{:S(2)}) copy-start(f32[2,1536]{1,0:T(2,128)} %copy-done.63) | copy-start | bytes 36868
  1235.8 260.9 %all-reduce.27.cloned.1.call-start = ((), (), s32[]{:S(2)}) async-start(), calls=%async_computation.8 | async-start | bytes 393216 | tf_op jit(solution)/shard_map/psum | solution.py:182
  1319.1 7.6 collective-permute-start.6
  1415.8 83.1 %copy-start.77 = (f32[2,1536]{1,0:T(2,128)S(1)}, f32[2,1536]{1,0:T(2,128)}, u32[]{:S(2)}) copy-start(f32[2,1536]{1,0:T(2,128)} %get-tuple-element.117) | copy-start | bytes 36868
  1415.8 83.1 %copy-start.82 = (f32[2,1536]{1,0:T(2,128)S(1)}, f32[2,1536]{1,0:T(2,128)}, u32[]{:S(2)}) copy-start(f32[2,1536]{1,0:T(2,128)} %get-tuple-element.118) | copy-start | bytes 36868
  1415.8 170.6 %all-reduce.29.cloned.1.call-start = ((), (), s32[]{:S(2)}) async-start(), calls=%async_computation.9 | async-start | bytes 393216 | tf_op jit(solution)/shard_map/psum | solution.py:196
  1500.7 85.7 %copy-start.72 = (f32[2,1,1536]{2,0,1:T(2,128)S(1)}, f32[2,1,1536]{2,0,1:T(2,128)}, u32[]{:S(2)}) copy-start(f32[2,1,1536]{2,0,1:T(2,128)} %copy.408) | copy-start | bytes 36868
  1504.3 85.2 %copy-start.97 = (f32[2,1536]{1,0:T(2,128)S(1)}, f32[2,1536]{1,0:T(2,128)}, u32[]{:S(2)}) copy-start(f32[2,1536]{1,0:T(2,128)} %get-tuple-element.121) | copy-start | bytes 36868
  1591.9 7.4 collective-permute-start.8
  (77 other events, 1718.2 us)
Sparse Core Ops, SparseCore 0:
  9.7 28.3 all-gather.3
  183.4 85.3 all-reduce.10
  276.6 81.8 all-reduce.12
  505.0 83.3 all-reduce.14
  596.2 81.8 all-reduce.16
  824.9 83.3 all-reduce.18
  916.0 81.8 all-reduce.20
  1144.7 83.3 all-reduce.22
  1235.9 81.8 all-reduce.24
  1415.9 80.6 all-reduce.26
  1504.5 81.8 all-reduce.28
where the time goes:
time: 1620 us; the launch traced here: 1610 us
  waiting for transfers between devices  784 us (48%)
  blocking collectives  481 us (30%)
  local copies, waits for them, and re-layouts  130 us (8%)
  matrix products  100 us (6%)
  other arithmetic  72.3 us (4%)
  between operations  25.4 us (2%)
    psum x5, waiting for transfers between devices, on_device(): lax.psum(jnp.dot(image_hidden, down_image[0], preferred_element_type=jnp....  404 us
    psum x5, waiting for transfers between devices, on_device(): lax.psum(image_part.astype(jnp.bfloat16), 'tp').astype(jnp.float32)  349 us
    psum x5, blocking collectives, on_device(): lax.psum(text_part.astype(jnp.bfloat16), 'tp').astype(jnp.float32)  201 us
    psum x5, blocking collectives, on_device(): lax.psum(jnp.dot(text_hidden_rows, down_text[0], preferred_element_type=j...  198 us
    all_gather x5, blocking collectives, on_device(): fresh_all = lax.all_gather(fresh_local, 'seq', axis=1, tiled=True)  67.8 us
  transfers between devices with their start and end apart: 20, of which 18 were waited for; matrix products, arithmetic and copies ran while one was open for 5% of the time, Pallas kernels for 0%

commit v1 on v0

--- a/solution.py
+++ b/solution.py
@@ -180,7 +180,9 @@
         text_flat = text_rows.reshape(-1, model_width).astype(jnp.float32)
         image_sum, text_sum = (
             lax.psum(image_part.astype(jnp.bfloat16), "tp").astype(jnp.float32),
-            lax.psum(text_part.astype(jnp.bfloat16), "tp").astype(jnp.float32),
+            jnp.sum(lax.all_gather(text_part.astype(jnp.bfloat16), "tp"), axis=0).astype(
+                jnp.float32
+            ),
         )
         image_first = image_flat + image_mrows[2] * image_sum
         text_first = text_flat + text_mrows[2] * text_sum

time: 1620 us -> 1570 us (0.969)
  waiting for transfers between devices: 784 us -> 738 us
    psum x5 -> x0, blocking collectives: 201 us -> none  [on_device(): lax.psum(text_part.astype(jnp.bfloat16), 'tp').astype(jnp.float32)]
    all_gather x0 -> x5, blocking collectives: none -> 187 us  [on_device(): lax.all_gather(text_part.astype(jnp.bfloat16), 'tp')]
    psum x5, waiting for transfers between devices: 349 us -> 299 us  [on_device(): lax.psum(image_part.astype(jnp.bfloat16), 'tp').astype(jnp.float32)]
  transfers between devices with their start and end apart: 20 -> 20, of which waited for: 18 -> 17; matrix products, arithmetic and copies ran while one was open for 5% -> 5% of each run, Pallas kernels for 0% -> 0%
where the time goes in v1:
time: 1570 us; the launch traced here: 1560 us
  waiting for transfers between devices  738 us (47%)
  blocking collectives  474 us (30%)
  local copies, waits for them, and re-layouts  127 us (8%)
  matrix products  100 us (6%)
  other arithmetic  77 us (5%)
  between operations  25.5 us (2%)
    psum x5, waiting for transfers between devices, on_device(): lax.psum(jnp.dot(image_hidden, down_image[0], preferred_element_type=jnp....  402 us
    psum x5, waiting for transfers between devices, on_device(): lax.psum(image_part.astype(jnp.bfloat16), 'tp').astype(jnp.float32)  299 us
    psum x5, blocking collectives, on_device(): lax.psum(jnp.dot(text_hidden_rows, down_text[0], preferred_element_type=j...  205 us
    all_gather x5, blocking collectives, on_device(): lax.all_gather(text_part.astype(jnp.bfloat16), 'tp')  187 us
    all_gather x5, blocking collectives, on_device(): fresh_all = lax.all_gather(fresh_local, 'seq', axis=1, tiled=True)  67.8 us
    ppermute x9, waiting for transfers between devices, passed_along(): lax.ppermute(value, axis, [(source, source + steps) for source in range(i...  37 us
  transfers between devices with their start and end apart: 20, of which 17 were waited for; matrix products, arithmetic and copies ran while one was open for 5% of the time, Pallas kernels for 0%

profile of v1, /device:TPU:2, one launch (start us, length us, event | category | flops | bytes accessed | tf_op | source)
XLA Modules:
  0.0 1556.7 jit_solution(11641508024709798911)
XLA Ops:
  24.7 14.3 all-gather.1
  40.0 13.2 all_gather.52
  94.3 36.8 %all-gather.2 = bf16[128,1536]{1,0:T(8,128)(2,1)S(1)} all-gather(bf16[16,1536]{1,0:T(8,128)(2,1)S(1)} %convolution_convert_fusion.9), channel_id=4, replica_groups=mesh['section'=2,'seq'=8,'tp'=8] {'tp'}, dimensions={0}, use_global_device_ids=true | all-gather | bytes 442368 | tf_op jit(solution)/shard_map/all_gather | solution.py:183
  131.6 3.4 fusion.55
  135.0 42.2 %psum.107 = bf16[16,1536]{1,0:T(8,128)(2,1)} all-reduce(bf16[16,1536]{1,0:T(8,128)(2,1)S(1)} %fusion.55), channel_id=1, replica_groups=mesh['section'=2,'seq'=8,'tp'=8] {'tp'}, use_global_device_ids=true, to_apply=%region_17.18 | all-reduce | flops 24576 | bytes 98304 | tf_op jit(solution)/shard_map/psum | solution.py:204
  181.8 3.2 collective-permute-done.1
  189.7 74.1 %all-reduce.11.cloned.1.call-done = bf16[64,1536]{1,0:T(8,128)(2,1)} async-done(((bf16[64,1536]{1,0:T(8,128)(2,1)}), bf16[64,1536]{1,0:T(8,128)(2,1)}) %all-reduce.11.cloned.1.call-update) | async-done | bytes 196624 | tf_op jit(solution)/shard_map/psum | solution.py:182
  267.8 3.6 fusion.40
  271.6 81.9 %all-reduce.13.cloned.1.call-done = bf16[64,1536]{1,0:T(8,128)(2,1)} async-done(((bf16[64,1536]{1,0:T(8,128)(2,1)}), bf16[64,1536]{1,0:T(8,128)(2,1)}) %all-reduce.13.cloned.1.call-update) | async-done | bytes 196624 | tf_op jit(solution)/shard_map/psum | solution.py:198
  356.6 5.7 collective-permute-done
  367.8 13.6 all_gather.56
  391.4 3.0 fusion.609
  410.8 37.5 %all-gather.3 = bf16[128,1536]{1,0:T(8,128)(2,1)} all-gather(bf16[16,1536]{1,0:T(8,128)(2,1)S(1)} %convolution_convert_fusion.8), channel_id=5, replica_groups=mesh['section'=2,'seq'=8,'tp'=8] {'tp'}, dimensions={0}, use_global_device_ids=true | all-gather | bytes 442368 | tf_op jit(solution)/shard_map/all_gather | solution.py:183
  449.6 4.0 fusion.58
  453.6 40.9 %psum.110 = bf16[16,1536]{1,0:T(8,128)(2,1)} all-reduce(bf16[16,1536]{1,0:T(8,128)(2,1)} %fusion.58), channel_id=1, replica_groups=mesh['section'=2,'seq'=8,'tp'=8] {'tp'}, use_global_device_ids=true, to_apply=%region_33.34 | all-reduce | flops 24576 | bytes 98304 | tf_op jit(solution)/shard_map/psum | solution.py:204
  499.0 3.1 collective-permute-done.3
  506.8 74.8 %all-reduce.15.cloned.1.call-done = bf16[64,1536]{1,0:T(8,128)(2,1)} async-done(((bf16[64,1536]{1,0:T(8,128)(2,1)}), bf16[64,1536]{1,0:T(8,128)(2,1)}) %all-reduce.15.cloned.1.call-update) | async-done | bytes 196624 | tf_op jit(solution)/shard_map/psum | solution.py:182
  585.6 3.6 fusion.43
  590.7 80.7 %all-reduce.17.cloned.1.call-done = bf16[64,1536]{1,0:T(8,128)(2,1)} async-done(((bf16[64,1536]{1,0:T(8,128)(2,1)}), bf16[64,1536]{1,0:T(8,128)(2,1)}) %all-reduce.17.cloned.1.call-update) | async-done | bytes 196624 | tf_op jit(solution)/shard_map/psum | solution.py:198
  674.0 6.2 collective-permute-done.2
  685.7 13.8 all_gather.59
  709.4 3.0 fusion.608
  728.8 37.5 %all-gather.4 = bf16[128,1536]{1,0:T(8,128)(2,1)} all-gather(bf16[16,1536]{1,0:T(8,128)(2,1)S(1)} %convolution_convert_fusion.7), channel_id=6, replica_groups=mesh['section'=2,'seq'=8,'tp'=8] {'tp'}, dimensions={0}, use_global_device_ids=true | all-gather | bytes 442368 | tf_op jit(solution)/shard_map/all_gather | solution.py:183
  767.7 4.0 fusion.61
  771.7 40.9 %psum.113 = bf16[16,1536]{1,0:T(8,128)(2,1)} all-reduce(bf16[16,1536]{1,0:T(8,128)(2,1)} %fusion.61), channel_id=1, replica_groups=mesh['section'=2,'seq'=8,'tp'=8] {'tp'}, use_global_device_ids=true, to_apply=%region_49.50 | all-reduce | flops 24576 | bytes 98304 | tf_op jit(solution)/shard_map/psum | solution.py:204
  817.1 3.1 collective-permute-done.5
  824.9 74.7 %all-reduce.19.cloned.1.call-done = bf16[64,1536]{1,0:T(8,128)(2,1)} async-done(((bf16[64,1536]{1,0:T(8,128)(2,1)}), bf16[64,1536]{1,0:T(8,128)(2,1)}) %all-reduce.19.cloned.1.call-update) | async-done | bytes 196624 | tf_op jit(solution)/shard_map/psum | solution.py:182
  903.6 3.6 fusion.46
  908.6 80.7 %all-reduce.21.cloned.1.call-done = bf16[64,1536]{1,0:T(8,128)(2,1)} async-done(((bf16[64,1536]{1,0:T(8,128)(2,1)}), bf16[64,1536]{1,0:T(8,128)(2,1)}) %all-reduce.21.cloned.1.call-update) | async-done | bytes 196624 | tf_op jit(solution)/shard_map/psum | solution.py:198
  991.9 6.2 collective-permute-done.4
  1003.6 13.6 all_gather.62
  1027.1 3.0 fusion.607
  1046.5 37.5 %all-gather.5 = bf16[128,1536]{1,0:T(8,128)(2,1)} all-gather(bf16[16,1536]{1,0:T(8,128)(2,1)S(1)} %convolution_convert_fusion.6), channel_id=7, replica_groups=mesh['section'=2,'seq'=8,'tp'=8] {'tp'}, dimensions={0}, use_global_device_ids=true | all-gather | bytes 442368 | tf_op jit(solution)/shard_map/all_gather | solution.py:183
  1085.4 4.0 fusion.64
  1089.4 41.1 %psum.116 = bf16[16,1536]{1,0:T(8,128)(2,1)} all-reduce(bf16[16,1536]{1,0:T(8,128)(2,1)} %fusion.64), channel_id=1, replica_groups=mesh['section'=2,'seq'=8,'tp'=8] {'tp'}, use_global_device_ids=true, to_apply=%region_65.66 | all-reduce | flops 24576 | bytes 98304 | tf_op jit(solution)/shard_map/psum | solution.py:204
  1135.0 3.1 collective-permute-done.7
  1142.1 75.4 %all-reduce.23.cloned.1.call-done = bf16[64,1536]{1,0:T(8,128)(2,1)} async-done(((bf16[64,1536]{1,0:T(8,128)(2,1)}), bf16[64,1536]{1,0:T(8,128)(2,1)}) %all-reduce.23.cloned.1.call-update) | async-done | bytes 196624 | tf_op jit(solution)/shard_map/psum | solution.py:182
  1221.5 3.6 fusion.49
  1227.4 79.9 %all-reduce.25.cloned.1.call-done = bf16[64,1536]{1,0:T(8,128)(2,1)} async-done(((bf16[64,1536]{1,0:T(8,128)(2,1)}), bf16[64,1536]{1,0:T(8,128)(2,1)}) %all-reduce.25.cloned.1.call-update) | async-done | bytes 196624 | tf_op jit(solution)/shard_map/psum | solution.py:198
  1309.9 6.2 collective-permute-done.6
  1321.6 13.6 all_gather.65
  1343.4 3.0 fusion.606
  1364.8 37.7 %all-gather.6 = bf16[128,1536]{1,0:T(8,128)(2,1)} all-gather(bf16[16,1536]{1,0:T(8,128)(2,1)S(1)} %convolution_convert_fusion.5), channel_id=8, replica_groups=mesh['section'=2,'seq'=8,'tp'=8] {'tp'}, dimensions={0}, use_global_device_ids=true | all-gather | bytes 442368 | tf_op jit(solution)/shard_map/all_gather | solution.py:183
  1403.9 4.0 fusion.67
  1407.9 40.1 %psum.119 = bf16[16,1536]{1,0:T(8,128)(2,1)S(1)} all-reduce(bf16[16,1536]{1,0:T(8,128)(2,1)} %fusion.67), channel_id=1, replica_groups=mesh['section'=2,'seq'=8,'tp'=8] {'tp'}, use_global_device_ids=true, to_apply=%region_81.82 | all-reduce | flops 24576 | bytes 98304 | tf_op jit(solution)/shard_map/psum | solution.py:204
  1452.1 3.6 fusion.52
  1457.2 79.0 %all-reduce.29.cloned.1.call-done = bf16[64,1536]{1,0:T(8,128)(2,1)} async-done(((bf16[64,1536]{1,0:T(8,128)(2,1)}), bf16[64,1536]{1,0:T(8,128)(2,1)}) %all-reduce.29.cloned.1.call-update) | async-done | bytes 196624 | tf_op jit(solution)/shard_map/psum | solution.py:198
  1541.7 3.4 collective-permute-start.8
  (568 shorter events, 265.9 us)
Async XLA Ops:
  7.2 260.6 %copy-start = (bf16[1,768,1536]{2,1,0:T(8,128)(2,1)S(1)}, bf16[1,768,1536]{2,1,0:T(8,128)(2,1)}, u32[]{:S(2)}) copy-start(bf16[1,768,1536]{2,1,0:T(8,128)(2,1)} %param.36) | copy-start | bytes 7077892
  7.2 73.3 %all-gather.9.cloned.1.call-start = ((), (), s32[]{:S(2)}) async-start(), calls=%async_computation.10 | async-start | bytes 2359296 | tf_op jit(solution)/shard_map/all_gather | solution.py:114
  9.2 254.5 %all-reduce.11.cloned.1.call-start = ((), (), s32[]{:S(2)}) async-start(), calls=%async_computation | async-start | bytes 393216 | tf_op jit(solution)/shard_map/psum | solution.py:182
  22.4 163.7 %copy-start.33 = (f32[2,1536]{1,0:T(2,128)}, f32[2,1536]{1,0:T(2,128)S(1)}, u32[]{:S(2)}) copy-start(f32[2,1536]{1,0:T(2,128)S(1)} %get-tuple-element.115) | copy-start | bytes 36868
  135.0 131.0 %copy-start.62 = (f32[2,1536]{1,0:T(2,128)S(1)}, f32[2,1536]{1,0:T(2,128)}, u32[]{:S(2)}) copy-start(f32[2,1536]{1,0:T(2,128)} %get-tuple-element.117) | copy-start | bytes 36868
  135.0 131.0 %copy-start.67 = (f32[2,1536]{1,0:T(2,128)S(1)}, f32[2,1536]{1,0:T(2,128)}, u32[]{:S(2)}) copy-start(f32[2,1536]{1,0:T(2,128)} %get-tuple-element.118) | copy-start | bytes 36868
  178.7 6.3 collective-permute-start.1
  181.7 82.0 %copy-start.12 = (bf16[2,128,1536]{2,1,0:T(8,128)(2,1)S(1)}, bf16[2,128,1536]{2,1,0:T(8,128)(2,1)}, u32[]{:S(2)}) copy-start(bf16[2,128,1536]{2,1,0:T(8,128)(2,1)} %param.21) | copy-start | bytes 2359300
  181.7 171.8 %all-reduce.13.cloned.1.call-start = ((), (), s32[]{:S(2)}) async-start(), calls=%async_computation.1 | async-start | bytes 393216 | tf_op jit(solution)/shard_map/psum | solution.py:198
  188.3 77.7 %copy-start.83 = (bf16[2,8,3,192]{3,2,1,0:T(4,128)(2,1)}, bf16[2,8,3,192]{3,2,1,0:T(4,128)(2,1)S(1)}, u32[]{:S(2)}) copy-start(bf16[2,8,3,192]{3,2,1,0:T(4,128)(2,1)S(1)} %reshape.1228) | copy-start | bytes 55300
  267.8 85.7 %copy-start.13 = (bf16[64,1536]{1,0:T(8,128)(2,1)S(1)}, bf16[64,1536]{1,0:T(8,128)(2,1)}, u32[]{:S(2)}) copy-start(bf16[64,1536]{1,0:T(8,128)(2,1)} %all-reduce.11.cloned.1.call-done) | copy-start | bytes 589828
  267.8 85.7 %copy-start.57 = (f32[2,1,1536]{2,0,1:T(2,128)S(1)}, f32[2,1,1536]{2,0,1:T(2,128)}, u32[]{:S(2)}) copy-start(f32[2,1,1536]{2,0,1:T(2,128)} %copy.408) | copy-start | bytes 36868
  271.4 92.2 %copy-start.48 = (f32[2,1536]{1,0:T(2,128)S(1)}, f32[2,1536]{1,0:T(2,128)}, u32[]{:S(2)}) copy-start(f32[2,1536]{1,0:T(2,128)} %copy-done.47) | copy-start | bytes 36868
  271.4 92.2 %copy-start.53 = (f32[2,1536]{1,0:T(2,128)S(1)}, f32[2,1536]{1,0:T(2,128)}, u32[]{:S(2)}) copy-start(f32[2,1536]{1,0:T(2,128)} %copy-done.52) | copy-start | bytes 36868
  271.4 310.2 %all-reduce.15.cloned.1.call-start = ((), (), s32[]{:S(2)}) async-start(), calls=%async_computation.2 | async-start | bytes 393216 | tf_op jit(solution)/shard_map/psum | solution.py:182
  271.6 92.2 %copy-start.27 = (bf16[2,4,8,2,192]{4,3,2,0,1:T(2,128)(2,1)}, bf16[2,4,8,2,192]{4,3,2,0,1:T(2,128)(2,1)S(1)}, u32[]{:S(2)}) copy-start(bf16[2,4,8,2,192]{4,3,2,0,1:T(2,128)(2,1)S(1)} %fusion.552) | copy-start | bytes 147460
  354.7 7.6 collective-permute-start
  453.6 130.2 %copy-start.63 = (f32[2,1536]{1,0:T(2,128)S(1)}, f32[2,1536]{1,0:T(2,128)}, u32[]{:S(2)}) copy-start(f32[2,1536]{1,0:T(2,128)} %get-tuple-element.117) | copy-start | bytes 36868
  453.6 130.2 %copy-start.68 = (f32[2,1536]{1,0:T(2,128)S(1)}, f32[2,1536]{1,0:T(2,128)}, u32[]{:S(2)}) copy-start(f32[2,1536]{1,0:T(2,128)} %get-tuple-element.118) | copy-start | bytes 36868
  496.0 6.2 collective-permute-start.3
  499.0 172.4 %all-reduce.17.cloned.1.call-start = ((), (), s32[]{:S(2)}) async-start(), calls=%async_computation.3 | async-start | bytes 393216 | tf_op jit(solution)/shard_map/psum | solution.py:198
  585.6 85.7 %copy-start.58 = (f32[2,1,1536]{2,0,1:T(2,128)S(1)}, f32[2,1,1536]{2,0,1:T(2,128)}, u32[]{:S(2)}) copy-start(f32[2,1,1536]{2,0,1:T(2,128)} %copy.408) | copy-start | bytes 36868
  589.2 92.2 %copy-start.49 = (f32[2,1536]{1,0:T(2,128)S(1)}, f32[2,1536]{1,0:T(2,128)}, u32[]{:S(2)}) copy-start(f32[2,1536]{1,0:T(2,128)} %copy-done.47) | copy-start | bytes 36868
  589.2 92.2 %copy-start.54 = (f32[2,1536]{1,0:T(2,128)S(1)}, f32[2,1536]{1,0:T(2,128)}, u32[]{:S(2)}) copy-start(f32[2,1536]{1,0:T(2,128)} %copy-done.52) | copy-start | bytes 36868
  589.3 310.3 %all-reduce.19.cloned.1.call-start = ((), (), s32[]{:S(2)}) async-start(), calls=%async_computation.4 | async-start | bytes 393216 | tf_op jit(solution)/shard_map/psum | solution.py:182
  672.6 7.6 collective-permute-start.2
  771.7 130.1 %copy-start.64 = (f32[2,1536]{1,0:T(2,128)S(1)}, f32[2,1536]{1,0:T(2,128)}, u32[]{:S(2)}) copy-start(f32[2,1536]{1,0:T(2,128)} %get-tuple-element.117) | copy-start | bytes 36868
  771.7 130.1 %copy-start.69 = (f32[2,1536]{1,0:T(2,128)S(1)}, f32[2,1536]{1,0:T(2,128)}, u32[]{:S(2)}) copy-start(f32[2,1536]{1,0:T(2,128)} %get-tuple-element.118) | copy-start | bytes 36868
  814.1 6.2 collective-permute-start.5
  817.1 172.2 %all-reduce.21.cloned.1.call-start = ((), (), s32[]{:S(2)}) async-start(), calls=%async_computation.5 | async-start | bytes 393216 | tf_op jit(solution)/shard_map/psum | solution.py:198
  903.6 85.7 %copy-start.59 = (f32[2,1,1536]{2,0,1:T(2,128)S(1)}, f32[2,1,1536]{2,0,1:T(2,128)}, u32[]{:S(2)}) copy-start(f32[2,1,1536]{2,0,1:T(2,128)} %copy.408) | copy-start | bytes 36868
  907.2 92.2 %copy-start.50 = (f32[2,1536]{1,0:T(2,128)S(1)}, f32[2,1536]{1,0:T(2,128)}, u32[]{:S(2)}) copy-start(f32[2,1536]{1,0:T(2,128)} %copy-done.47) | copy-start | bytes 36868
  907.2 92.2 %copy-start.55 = (f32[2,1536]{1,0:T(2,128)S(1)}, f32[2,1536]{1,0:T(2,128)}, u32[]{:S(2)}) copy-start(f32[2,1536]{1,0:T(2,128)} %copy-done.52) | copy-start | bytes 36868
  907.2 310.3 %all-reduce.23.cloned.1.call-start = ((), (), s32[]{:S(2)}) async-start(), calls=%async_computation.6 | async-start | bytes 393216 | tf_op jit(solution)/shard_map/psum | solution.py:182
  990.5 7.6 collective-permute-start.4
  1089.4 130.3 %copy-start.65 = (f32[2,1536]{1,0:T(2,128)S(1)}, f32[2,1536]{1,0:T(2,128)}, u32[]{:S(2)}) copy-start(f32[2,1536]{1,0:T(2,128)} %get-tuple-element.117) | copy-start | bytes 36868
  1089.4 130.3 %copy-start.70 = (f32[2,1536]{1,0:T(2,128)S(1)}, f32[2,1536]{1,0:T(2,128)}, u32[]{:S(2)}) copy-start(f32[2,1536]{1,0:T(2,128)} %get-tuple-element.118) | copy-start | bytes 36868
  1132.0 6.2 collective-permute-start.7
  1135.0 172.3 %all-reduce.25.cloned.1.call-start = ((), (), s32[]{:S(2)}) async-start(), calls=%async_computation.7 | async-start | bytes 393216 | tf_op jit(solution)/shard_map/psum | solution.py:198
  1221.5 85.7 %copy-start.60 = (f32[2,1,1536]{2,0,1:T(2,128)S(1)}, f32[2,1,1536]{2,0,1:T(2,128)}, u32[]{:S(2)}) copy-start(f32[2,1,1536]{2,0,1:T(2,128)} %copy.408) | copy-start | bytes 36868
  1225.1 92.2 %copy-start.51 = (f32[2,1536]{1,0:T(2,128)S(1)}, f32[2,1536]{1,0:T(2,128)}, u32[]{:S(2)}) copy-start(f32[2,1536]{1,0:T(2,128)} %copy-done.47) | copy-start | bytes 36868
  1225.1 92.2 %copy-start.56 = (f32[2,1536]{1,0:T(2,128)S(1)}, f32[2,1536]{1,0:T(2,128)}, u32[]{:S(2)}) copy-start(f32[2,1536]{1,0:T(2,128)} %copy-done.52) | copy-start | bytes 36868
  1225.2 222.9 %all-reduce.27.cloned.1.call-start = ((), (), s32[]{:S(2)}) async-start(), calls=%async_computation.8 | async-start | bytes 393216 | tf_op jit(solution)/shard_map/psum | solution.py:182
  1308.5 7.6 collective-permute-start.6
  1364.7 171.5 %all-reduce.29.cloned.1.call-start = ((), (), s32[]{:S(2)}) async-start(), calls=%async_computation.9 | async-start | bytes 393216 | tf_op jit(solution)/shard_map/psum | solution.py:198
  1452.1 84.1 %copy-start.61 = (f32[2,1,1536]{2,0,1:T(2,128)S(1)}, f32[2,1,1536]{2,0,1:T(2,128)}, u32[]{:S(2)}) copy-start(f32[2,1,1536]{2,0,1:T(2,128)} %copy.408) | copy-start | bytes 36868
  1455.7 83.6 %copy-start.96 = (f32[2,1536]{1,0:T(2,128)S(1)}, f32[2,1536]{1,0:T(2,128)}, u32[]{:S(2)}) copy-start(f32[2,1536]{1,0:T(2,128)} %get-tuple-element.121) | copy-start | bytes 36868
  1541.7 7.4 collective-permute-start.8
  (75 other events, 1656.7 us)
Sparse Core Ops, SparseCore 0:
  9.7 28.3 all-gather.8
  181.9 81.8 all-reduce.10
  271.6 81.8 all-reduce.12
  499.1 82.4 all-reduce.14
  589.4 81.8 all-reduce.16
  817.2 82.3 all-reduce.18
  907.3 81.8 all-reduce.20
  1135.1 82.3 all-reduce.22
  1225.3 81.8 all-reduce.24
  1364.8 81.2 all-reduce.26
  1455.9 80.3 all-reduce.28
